TPU v7x, 32 devices: a whole 2x2x4 slice. The times are simulated.
32 devices in a mesh: exp: 4 (over x, core), seq: 8 (over z, y).
Axes of the slice: x: 2, y: 2, z: 4, core: 2. Of those that a mesh axis runs over, the one named last changes fastest.
Arguments:
- hidden_in: bfloat16 [2048, 4096], P(('exp', 'seq')), may hold values from -3 to 3
- doc_ids: int32 [2048], P(('exp', 'seq')), may hold values from 0 to 31, never falling along the last dimension, each value on 1 to 256 neighbouring positions
- attn_gain: float32 [4096], replicated, may hold values from 0.1 to 1.9
- q_weight: bfloat16 [4096, 4096], P('exp', 'seq'), may hold values from -0.09375 to 0.09375
- kv_weight: bfloat16 [4, 4096, 256], P(None, 'exp'), may hold values from -0.09375 to 0.09375
- q_gain: float32 [128], replicated, may hold values from 0.5 to 5, as said below
- k_gain: float32 [128], replicated, may hold values from 0.5 to 5, as said below
- out_weight: bfloat16 [4096, 4096], P('seq', 'exp'), may hold values from -0.25 to 0.25
- ffn_gain: float32 [4096], replicated, may hold values from 0.1 to 1.9
- router_weight: bfloat16 [4096, 32], replicated, may hold values from -0.0234375 to 0.0234375
- routes: int32 [2048, 8], P(('exp', 'seq')), may hold values from 0 to 31, all different within a row; in each aligned block of 64 rows (0 to 63, 64 to 127, ...) at most 32 rows name the same one
- expert_in: bfloat16 [32, 4096, 1536], P(('exp', 'seq')), may hold values from -0.09375 to 0.09375
- expert_out: bfloat16 [32, 768, 4096], P(('exp', 'seq')), may hold values from -0.875 to 0.875
Outputs:
- layer_out: bfloat16 [2048, 4096], P(('exp', 'seq'))
Inputs may be any that keep to these rules, and one draw needn't show every extreme that they name: `routes`: each row names 8 different experts. Among the rows of one device no expert is named by more than 32 rows, a bound that some block reaches. `doc_ids`: never falls along the tokens; each document has 1 to 256 tokens, one has exactly 256. `q_gain`: Positive. `k_gain`: Positive.
All inputs are finite; a program needn't handle non-finite values.
Results may differ from a plain program's by a relative error of at most 0.019.
The roundings to bfloat16 on the way count: a program that leaves them out, or rounds other values in their place, can miss the bound.
Values may be sent and summed in bfloat16 or wider, within the bound.
No kernel may reach another device: no remote copies, remote signals or barrier semaphores. Data moves between devices by JAX's collectives and lax.ppermute only.
A program may use at most 128 MiB of HBM per device.

v0:
```python
import math

import jax
import jax.numpy as jnp
from jax import lax
from jax.sharding import PartitionSpec as P

HEADS = 32
KV = 4
HD = 128
TOPK = 8


def rms_scale(values, gain):
    return values * lax.rsqrt(jnp.mean(values * values, axis=-1, keepdims=True) + 1e-06) * gain


def rotate(values, position):
    half = values.shape[-1] // 2
    freq = jnp.exp(
        -(2.0 * jnp.arange(half, dtype=jnp.float32) / values.shape[-1]) * math.log(1000000.0)
    )
    angle = position[:, None, None] * freq
    cosine = jnp.cos(angle)
    sine = jnp.sin(angle)
    first = values[..., :half]
    second = values[..., half:]
    return jnp.concatenate(
        [first * cosine - second * sine, second * cosine + first * sine], axis=-1
    )


def attend(queries, keys, values, position, docs):
    length = keys.shape[0]
    block = min(512, length)
    count = length // block
    scale = 1.0 / math.sqrt(keys.shape[-1])

    def one_block(items):
        query_block, query_pos, query_docs = items
        scores = (
            jnp.einsum("qhd,kd->hqk", query_block, keys, preferred_element_type=jnp.float32) * scale
        )
        allowed = (position[None, :] <= query_pos[:, None]) & (docs[None, :] == query_docs[:, None])
        scores = jnp.where(allowed[None], scores, -1e30)
        top = jnp.max(scores, axis=-1, keepdims=True)
        expo = jnp.exp(scores - top)
        weights = (expo / jnp.sum(expo, axis=-1, keepdims=True)).astype(jnp.bfloat16)
        return jnp.einsum(
            "hqk,kd->qhd", weights, values, preferred_element_type=jnp.float32
        ).astype(jnp.bfloat16)

    heads = queries.shape[1]
    out = lax.map(
        one_block,
        (
            queries.reshape(count, block, heads, -1),
            position.reshape(count, block),
            docs.reshape(count, block),
        ),
    )
    return out.reshape(length, -1)


def local(
    hidden_in,
    doc_ids,
    attn_gain,
    q_weight,
    kv_weight,
    q_gain,
    k_gain,
    out_weight,
    ffn_gain,
    router_weight,
    routes,
    expert_in,
    expert_out,
):
    heads_dev = q_weight.shape[1] // HD
    first_head = lax.axis_index("seq") * heads_dev
    kv_local = lax.dynamic_index_in_dim(kv_weight, first_head // (HEADS // KV), 0, keepdims=False)
    q_full, kv_full, out_full = (
        lax.all_gather(q_weight, "exp", axis=0, tiled=True),
        lax.all_gather(kv_local, "exp", axis=0, tiled=True),
        lax.all_gather(out_weight, "exp", axis=1, tiled=True),
    )
    normed = rms_scale(hidden_in.astype(jnp.float32), attn_gain).astype(jnp.bfloat16)
    seq_rows, seq_docs = (
        lax.all_gather(normed, "seq", axis=0, tiled=True),
        lax.all_gather(doc_ids, "seq", axis=0, tiled=True),
    )
    length = seq_rows.shape[0]
    position = jnp.arange(length, dtype=jnp.float32)
    queries = jnp.dot(seq_rows, q_full, preferred_element_type=jnp.float32).reshape(
        length, heads_dev, HD
    )
    queries = rotate(rms_scale(queries, q_gain), position).astype(jnp.bfloat16)
    pairs = jnp.dot(seq_rows, kv_full, preferred_element_type=jnp.float32)
    keys = rotate(rms_scale(pairs[:, None, :HD], k_gain), position)[:, 0].astype(jnp.bfloat16)
    values = pairs[:, HD:].astype(jnp.bfloat16)
    context = attend(queries, keys, values, position, seq_docs)
    tok_count = hidden_in.shape[0]
    attn_rows = lax.psum_scatter(
        jnp.dot(context, out_full, preferred_element_type=jnp.float32).astype(jnp.bfloat16),
        "seq",
        scatter_dimension=0,
        tiled=True,
    ).astype(jnp.float32)
    mid = (hidden_in.astype(jnp.float32) + attn_rows).astype(jnp.bfloat16)
    ffn_in = rms_scale(mid.astype(jnp.float32), ffn_gain).astype(jnp.bfloat16)
    experts = router_weight.shape[1]
    capacity = 2 * tok_count * TOPK // experts
    logits = jnp.dot(ffn_in, router_weight, preferred_element_type=jnp.float32)
    probs = jax.nn.softmax(logits, axis=-1)
    chosen = routes[:, :, None] == jnp.arange(experts, dtype=jnp.int32)[None, None, :]
    picked = jnp.sum(jnp.where(chosen, probs[:, None, :], 0.0), axis=-1)
    gates = picked / jnp.sum(picked, axis=-1, keepdims=True)
    flat_hot = chosen.reshape(tok_count * TOPK, experts).astype(jnp.int32)
    before = jnp.cumsum(flat_hot, axis=0) - flat_hot
    slots = jnp.sum(before * flat_hot, axis=-1).reshape(tok_count, TOPK)
    slot_hot = slots[:, :, None] == jnp.arange(capacity, dtype=jnp.int32)[None, None, :]
    placing = jnp.sum(
        (chosen[:, :, :, None] & slot_hot[:, :, None, :]).astype(jnp.bfloat16), axis=1
    )
    sending = jnp.einsum("tec,td->ecd", placing, ffn_in, preferred_element_type=jnp.float32).astype(
        jnp.bfloat16
    )
    received = lax.all_to_all(sending, ("exp", "seq"), split_axis=0, concat_axis=0, tiled=True)
    flat = received.reshape(-1, received.shape[-1])
    both = jnp.dot(flat, expert_in[0], preferred_element_type=jnp.float32)
    width = expert_out.shape[1]
    act = (jax.nn.silu(both[:, :width]) * both[:, width:]).astype(jnp.bfloat16)
    result = jnp.dot(act, expert_out[0], preferred_element_type=jnp.float32).astype(jnp.bfloat16)
    returned = lax.all_to_all(
        result.reshape(received.shape), ("exp", "seq"), split_axis=0, concat_axis=0, tiled=True
    )
    index = (routes * capacity + slots).reshape(-1)
    rows = jnp.take(returned.reshape(experts * capacity, -1), index, axis=0).reshape(
        tok_count, TOPK, -1
    )
    mixture = jnp.einsum("tk,tkd->td", gates, rows.astype(jnp.float32))
    return (mid.astype(jnp.float32) + mixture).astype(jnp.bfloat16)


def solution(mesh):
    in_specs = (
        P(("exp", "seq"), None),
        P(("exp", "seq")),
        P(),
        P("exp", "seq"),
        P(None, "exp", None),
        P(),
        P(),
        P("seq", "exp"),
        P(),
        P(),
        P(("exp", "seq"), None),
        P(("exp", "seq"), None, None),
        P(("exp", "seq"), None, None),
    )
    out_specs = P(("exp", "seq"), None)
    return jax.shard_map(local, mesh=mesh, in_specs=in_specs, out_specs=out_specs, check_vma=False)
```

profile of v0, /device:TPU:0, one launch (start us, length us, event | category | flops | bytes accessed | tf_op | source)
XLA Modules:
  0.0 710.0 jit_solution(9731205435401145940)
XLA Ops:
  6.5 0.7 all-gather.8.cloned.1.call-update
  7.3 1.2 fusion.19
  8.6 2.0 fusion.21
  10.7 0.9 constant_dynamic-slice_fusion
  11.6 0.5 all-gather.10.cloned.1.call-update
  12.2 0.6 dynamic-slice.2
  13.5 0.2 dynamic-update-slice
  13.8 13.1 %all-reduce = s32[512]{0:T(512)S(1)} all-reduce(s32[512]{0:T(512)S(1)} %dynamic-update-slice), channel_id=1, replica_groups=mesh['exp'=4,'seq'=8] {'seq'}, use_global_device_ids=true, to_apply=%add | all-reduce | flops 512 | bytes 4096
  26.9 0.3 fusion.27
  27.2 1.0 fusion.34
  28.2 17.9 %all-gather.8.cloned.1.call-done = bf16[4096,512]{1,0:T(8,128)(2,1)} async-done(((bf16[1024,512]{1,0:T(8,128)(2,1)}), bf16[4096,512]{1,0:T(8,128)(2,1)}) %all-gather.8.cloned.1.call-update) | async-done | bytes 4194320 | tf_op jit(solution)/shard_map/all_gather | solution.py:84
  46.1 75.0 %all-gather.6.cloned.1.call-done = bf16[512,4096]{1,0:T(8,128)(2,1)} async-done(((bf16[64,4096]{1,0:T(8,128)(2,1)}), bf16[512,4096]{1,0:T(8,128)(2,1)}) %all-gather.6.cloned.1.call-update) | async-done | bytes 4194320 | tf_op jit(solution)/shard_map/all_gather | solution.py:90
  121.1 5.9 multiply_reduce_fusion
  126.9 0.3 copy.40
  127.3 16.5 %all-gather.12.cloned.1.call-done = bf16[1,4096,256]{2,1,0:T(8,128)(2,1)} async-done(((bf16[1,1024,256]{2,1,0:T(8,128)(2,1)}), bf16[1,4096,256]{2,1,0:T(8,128)(2,1)}) %all-gather.12.cloned.1.call-update) | async-done | bytes 2097168 | tf_op jit(solution)/shard_map/all_gather | solution.py:85
  143.8 4.2 fusion.9
  148.0 0.1 multiply_bitcast_fusion
  148.1 0.6 fusion.47
  148.7 0.3 multiply_multiply_fusion
  149.0 0.4 subtract_convert_fusion
  149.5 0.8 fusion.28
  150.3 2.3 fusion.58
  152.6 0.5 fusion.18
  153.1 26.6 %all-gather.10.cloned.1.call-done = bf16[512,4096]{1,0:T(8,128)(2,1)} async-done(((bf16[512,1024]{1,0:T(8,128)(2,1)}), bf16[512,4096]{1,0:T(8,128)(2,1)}) %all-gather.10.cloned.1.call-update) | async-done | bytes 4194320 | tf_op jit(solution)/shard_map/all_gather | solution.py:86
  179.7 6.5 convolution_convert_fusion.2
  186.2 0.7 copy-done.3
  186.9 0.1 eq.87
  187.0 0.1 eq.83
  187.1 1.2 reduce-window.6
  188.3 0.2 slice_reduce_fusion
  188.6 0.1 fusion.46
  188.7 0.1 reshape.280
  188.9 0.7 fusion.8
  189.5 85.1 %reduce-scatter.2.cloned.1.call-done = bf16[64,4096]{1,0:T(8,128)(2,1)} async-done(((bf16[512,4096]{1,0:T(8,128)(2,1)}), bf16[64,4096]{1,0:T(8,128)(2,1)}) %reduce-scatter.2.cloned.1.call-update) | async-done | bytes 524304 | tf_op jit(solution)/shard_map/reduce_scatter | solution.py:104
  274.6 1.3 fusion.23
  276.0 2.4 convolution_convert_fusion.1
  278.4 188.8 %all_to_all.10 = bf16[32,32,4096]{2,1,0:T(8,128)(2,1)S(1)} all-to-all(bf16[32,32,4096]{2,1,0:T(8,128)(2,1)S(1)} %convolution_convert_fusion.1), channel_id=1, replica_groups=mesh['exp'=4,'seq'=8] {'exp','seq'}, dimensions={0} | all-to-all | bytes 16777216 | tf_op jit(solution)/shard_map/all_to_all | solution.py:129
  467.2 15.8 %fusion.1 = f32[1024,1536]{1,0:T(8,128)S(1)} fusion(bf16[1024,4096]{1,0:T(8,128)(2,1)S(1)} %bitcast.81, bf16[1,4096,1536]{2,1,0:T(8,128)(2,1)} %param.24), kind=kOutput, calls=%fused_computation.2 | convolution fusion | flops 12884901888 | bytes 27262976 | tf_op jit(solution)/shard_map/dot_general | solution.py:131
  483.1 8.9 %convolution_convert_fusion = bf16[1024,4096]{1,0:T(8,128)(2,1)} fusion(bf16[1,768,4096]{2,1,0:T(8,128)(2,1)S(1)} %bitcast.86, f32[1024,1536]{1,0:T(8,128)S(1)} %fusion.1), kind=kOutput, calls=%fused_computation.4 | convolution fusion | flops 6451363840 | bytes 20971520 | tf_op jit(solution)/shard_map/dot_general | solution.py:134
  492.0 4.1 all-to-all-start.1
  496.1 0.1 reshape.284
  496.2 0.1 copy.47
  496.4 0.4 fusion.59
  496.9 0.1 copy.52
  497.0 188.4 %all-to-all-done.1 = bf16[32,32,4096]{2,1,0:T(8,128)(2,1)} async-done(((bf16[32,32,4096]{2,1,0:T(8,128)(2,1)}), bf16[32,32,4096]{2,1,0:T(8,128)(2,1)}, u32[]{:S(2)}, u32[]{:S(2)}) %all-to-all-start.1) | async-done | bytes 8388640 | tf_op jit(solution)/shard_map/all_to_all | solution.py:135
  685.4 13.2 %gather_fusion = bf16[512,4096]{1,0:T(8,128)(2,1)} fusion(bf16[1024,4096]{1,0:T(8,128)(2,1)} %bitcast.18, s32[1024]{0:T(1024)S(1)} %pad_clamp_fusion), kind=kCustom, calls=%fused_computation | custom fusion | bytes 8390656 | tf_op jit(solution)/shard_map/jit(_take)/gather | solution.py:139
  698.6 3.5 fusion.4
  702.1 1.4 fusion.26
  (53 shorter events, 0.8 us)
Async XLA Ops:
  6.5 4.2 copy-start
  6.5 5.7 copy-start.9
  6.5 7.0 copy-start.8
  6.5 39.6 %all-gather.8.cloned.1.call-start = ((), (), s32[]{:S(2)}) async-start(), calls=%async_computation.4 | async-start | bytes 5242880 | tf_op jit(solution)/shard_map/all_gather | solution.py:84
  7.3 113.8 %all-gather.6.cloned.1.call-start = ((), (), s32[]{:S(2)}) async-start(), calls=%async_computation.3 | async-start | bytes 4718592 | tf_op jit(solution)/shard_map/all_gather | solution.py:90
  10.6 133.1 %all-gather.12.cloned.1.call-start = ((), (), s32[]{:S(2)}) async-start(), calls=%async_computation.7 | async-start | bytes 2621440 | tf_op jit(solution)/shard_map/all_gather | solution.py:85
  11.6 168.1 %all-gather.10.cloned.1.call-start = ((), (), s32[]{:S(2)}) async-start(), calls=%async_computation.5 | async-start | bytes 5242880 | tf_op jit(solution)/shard_map/all_gather | solution.py:86
  12.2 262.4 %reduce-scatter.2.cloned.1.call-start = ((), (), s32[]{:S(2)}) async-start(), calls=%async_computation.6 | async-start | bytes 4718592 | tf_op jit(solution)/shard_map/reduce_scatter | solution.py:104
  127.3 20.7 %copy-start.5 = (f32[128]{0:T(128)S(1)}, f32[128]{0:T(128)}, u32[]{:S(2)}) copy-start(f32[128]{0:T(128)} %param.19) | copy-start | bytes 1540
  127.3 21.4 %copy-start.6 = (f32[128]{0:T(128)S(1)}, f32[128]{0:T(128)}, u32[]{:S(2)}) copy-start(f32[128]{0:T(128)} %param.18) | copy-start | bytes 1540
  186.1 0.7 copy-start.3
  186.2 88.5 %copy-start.2 = (bf16[64,4096]{1,0:T(8,128)(2,1)S(1)}, bf16[64,4096]{1,0:T(8,128)(2,1)}, u32[]{:S(2)}) copy-start(bf16[64,4096]{1,0:T(8,128)(2,1)} %param.13) | copy-start | bytes 1572868
  186.2 89.8 %copy-start.4 = (f32[4096]{0:T(1024)S(1)}, f32[4096]{0:T(1024)}, u32[]{:S(2)}) copy-start(f32[4096]{0:T(1024)} %param.21) | copy-start | bytes 49156
  278.4 204.7 %slice-start = ((s8[6291456]{0:T(1024)(128)(4,1)}), s8[2097152]{0:T(1024)(128)(4,1)S(1)}, s32[]{:S(2)}) async-start(s8[6291456]{0:T(1024)(128)(4,1)} %bitcast.85), calls=%async_computation.8 | async-start | bytes 4194304
  467.2 15.8 %slice-start.1 = ((s8[6291456]{0:T(1024)(128)(4,1)}), s8[4194304]{0:T(1024)(128)(4,1)S(1)}, s32[]{:S(2)}) async-start(s8[6291456]{0:T(1024)(128)(4,1)} %bitcast.85), calls=%async_computation.9 | async-start | bytes 8388608
  492.0 4.4 copy-start.7
  492.0 193.4 %all-to-all-start.1 = ((bf16[32,32,4096]{2,1,0:T(8,128)(2,1)}), bf16[32,32,4096]{2,1,0:T(8,128)(2,1)}, u32[]{:S(2)}, u32[]{:S(2)}) async-start(bf16[32,32,4096]{2,1,0:T(8,128)(2,1)} %bitcast.80), calls=%async_computation.2 | async-start | bytes 16777216 | tf_op jit(solution)/shard_map/all_to_all | solution.py:135
  685.4 18.1 %copy-start.1 = (bf16[4,1024,256]{2,1,0:T(8,128)(2,1)S(1)}, bf16[4,1024,256]{2,1,0:T(8,128)(2,1)}, u32[]{:S(2)}) copy-start(bf16[4,1024,256]{2,1,0:T(8,128)(2,1)} %param.17) | copy-start | bytes 6291460
Sparse Core Ops, SparseCore 0:
  8.9 37.1 all-gather.7
  48.2 72.7 all-gather.5
  122.6 21.0 all-gather.11
  145.2 34.4 all-gather.9
  186.3 88.2 reduce-scatter.1
where the time goes:
time: 710 us
  waiting for transfers between devices  411 us (58%)
  blocking collectives  202 us (28%)
  matrix products  48.8 us (7%)
  local copies, waits for them, and re-layouts  17 us (2%)
  between operations  14.1 us (2%)
  other arithmetic  13.3 us (2%)
    all_to_all x1, blocking collectives, local(): lax.all_to_all(sending, ('exp', 'seq'), split_axis=0, concat_axis=0, tile...  189 us
    all_to_all x1, waiting for transfers between devices, local(): lax.all_to_all(result.reshape(received.shape), ('exp', 'seq'), split_axis...  188 us
    reduce_scatter x1, waiting for transfers between devices, local(): lax.psum_scatter(jnp.dot(context, out_full, preferred_element_type=jnp.fl...  85.1 us
    all_gather x1, waiting for transfers between devices, local(): lax.all_gather(normed, 'seq', axis=0, tiled=True)  75 us
    all_gather x1, waiting for transfers between devices, local(): lax.all_gather(out_weight, 'exp', axis=1, tiled=True)  26.6 us
    all_gather x1, waiting for transfers between devices, local(): lax.all_gather(q_weight, 'exp', axis=0, tiled=True)  17.9 us
    all_gather x1, waiting for transfers between devices, local(): lax.all_gather(kv_local, 'exp', axis=0, tiled=True)  16.5 us
    dot_general x1, matrix products, local(): both = jnp.dot(flat, expert_in[0], preferred_element_type=jnp.float32)  15.8 us
  transfers between devices with their start and end apart: 6, of which 6 were waited for; matrix products, arithmetic and copies ran while one was open for 4% of the time, Pallas kernels for 0%

commit v1 on v0

v1 whole, which is shorter than its diff:
```python
import functools
import math

import jax
import jax.numpy as jnp
from jax import lax
from jax.sharding import PartitionSpec as P

HEADS = 32
KV = 4
HD = 128
TOPK = 8


def rms_scale(values, gain):
    return values * lax.rsqrt(jnp.mean(values * values, axis=-1, keepdims=True) + 1e-06) * gain


def rotate(values, position):
    half = values.shape[-1] // 2
    freq = jnp.exp(
        -(2.0 * jnp.arange(half, dtype=jnp.float32) / values.shape[-1]) * math.log(1000000.0)
    )
    angle = position[:, None, None] * freq
    cosine = jnp.cos(angle)
    sine = jnp.sin(angle)
    first = values[..., :half]
    second = values[..., half:]
    return jnp.concatenate(
        [first * cosine - second * sine, second * cosine + first * sine], axis=-1
    )


def swap(values, axis, size, mask):
    return lax.ppermute(values, axis, [(i, i ^ mask) for i in range(size)])


def permute_blocks(values, own, count):
    width = values.shape[-1]
    bit = count // 2
    span = width // 2
    while bit > 0:
        parts = values.reshape(values.shape[:-1] + (width // (2 * span), 2, span))
        parts = jnp.where((own & bit) != 0, parts[..., ::-1, :], parts)
        values = parts.reshape(values.shape)
        bit //= 2
        span //= 2
    return values


def gather_pieces(shard, axis, size):
    pieces = []
    for far in range(size // 2):
        near = shard if far == 0 else swap(shard, axis, size, 2 * far)
        pieces += [near, swap(near, axis, size, 1)]
    return pieces


def attend(queries, keys, values, query_pos, query_docs, position, docs):
    scale = 1.0 / math.sqrt(keys.shape[-1])
    scores = jnp.einsum("qhd,kd->hqk", queries, keys, preferred_element_type=jnp.float32) * scale
    allowed = (position[None, :] <= query_pos[:, None]) & (docs[None, :] == query_docs[:, None])
    scores = jnp.where(allowed[None], scores, -1e30)
    top = jnp.max(scores, axis=-1, keepdims=True)
    expo = jnp.exp(scores - top)
    weights = (expo / jnp.sum(expo, axis=-1, keepdims=True)).astype(jnp.bfloat16)
    context = jnp.einsum(
        "hqk,kd->qhd", weights, values, preferred_element_type=jnp.float32
    ).astype(jnp.bfloat16)
    return context.reshape(queries.shape[0], -1)


def attention_rows(
    hidden_in, doc_ids, attn_gain, q_weight, kv_weight, q_gain, k_gain, out_weight, n_exp, n_seq
):
    own_exp = lax.axis_index("exp")
    own_seq = lax.axis_index("seq")
    heads_dev = q_weight.shape[1] // HD
    rows = hidden_in.shape[0]
    kv_local = lax.dynamic_index_in_dim(
        kv_weight, own_seq * heads_dev // (HEADS // KV), 0, keepdims=False
    )
    normed = rms_scale(hidden_in.astype(jnp.float32), attn_gain).astype(jnp.bfloat16)
    normed = permute_blocks(normed, own_exp, n_exp)
    blocks = gather_pieces(normed, "seq", n_seq)
    qkv_pieces = gather_pieces(jnp.concatenate([q_weight, kv_local], axis=1), "exp", n_exp)
    out_pieces = gather_pieces(out_weight, "exp", n_exp)
    qkv_full = jnp.concatenate(qkv_pieces, axis=0)
    out_full = jnp.concatenate(out_pieces, axis=1)

    order = own_seq ^ jnp.arange(n_seq, dtype=jnp.int32)
    all_docs = lax.all_gather(doc_ids, "seq", axis=0, tiled=False)
    docs = jnp.take(all_docs, order, axis=0).reshape(-1)
    position = (
        (order[:, None] * rows + jnp.arange(rows, dtype=jnp.int32)[None, :])
        .reshape(-1)
        .astype(jnp.float32)
    )
    q_width = heads_dev * HD
    queries, keys, values = [], [], []
    count = n_seq // 2
    for far in range(count):
        span = slice(2 * far * rows, 2 * (far + 1) * rows)
        tokens = jnp.concatenate(blocks[2 * far : 2 * far + 2], axis=0)
        mixed = jnp.dot(tokens, qkv_full, preferred_element_type=jnp.float32)
        query = mixed[:, :q_width].reshape(2 * rows, heads_dev, HD)
        queries.append(rotate(rms_scale(query, q_gain), position[span]).astype(jnp.bfloat16))
        key = mixed[:, None, q_width : q_width + HD]
        keys.append(rotate(rms_scale(key, k_gain), position[span])[:, 0].astype(jnp.bfloat16))
        values.append(mixed[:, q_width + HD :].astype(jnp.bfloat16))
    keys = jnp.concatenate(keys, axis=0)
    values = jnp.concatenate(values, axis=0)
    total = 0.0
    for far in reversed(range(count)):
        span = slice(2 * far * rows, 2 * (far + 1) * rows)
        context = attend(
            queries[far], keys, values, position[span], docs[span], position, docs
        )
        partial = jnp.dot(context, out_full, preferred_element_type=jnp.float32).astype(
            jnp.bfloat16
        )
        other = swap(partial[rows:], "seq", n_seq, 1)
        pair = partial[:rows].astype(jnp.float32) + other.astype(jnp.float32)
        if far > 0:
            pair = swap(pair.astype(jnp.bfloat16), "seq", n_seq, 2 * far).astype(jnp.float32)
        total = total + pair
    return permute_blocks(total, own_exp, n_exp)


def router_gates(ffn_in, router_weight, routes):
    experts = router_weight.shape[1]
    logits = jnp.dot(ffn_in, router_weight, preferred_element_type=jnp.float32)
    probs = jax.nn.softmax(logits, axis=-1)
    chosen = routes[:, :, None] == jnp.arange(experts, dtype=jnp.int32)[None, None, :]
    return probs, chosen


def experts_gathered(ffn_in, router_weight, routes, expert_in, expert_out, n_exp, n_seq):
    rows, depth = ffn_in.shape
    half = depth // 2
    experts = router_weight.shape[1]
    own_exp = lax.axis_index("exp")
    own_seq = lax.axis_index("seq")
    in_weights = [expert_in[0], swap(expert_in[0], "exp", n_exp, 1)]
    out_weights = [expert_out[0], swap(expert_out[0], "exp", n_exp, 1)]
    width = expert_out.shape[1]
    ids = [(own_exp ^ m) * n_seq + own_seq for m in range(2)]

    probs, chosen = router_gates(ffn_in, router_weight, routes)
    picked = jnp.where(jnp.any(chosen, axis=1), probs, 0.0)
    gates = picked / jnp.sum(picked, axis=-1, keepdims=True)
    gate_high = gates.astype(jnp.bfloat16)
    gate_low = (gates - gate_high.astype(jnp.float32)).astype(jnp.bfloat16)
    extra = jnp.concatenate([gate_high, gate_low], axis=1)
    extra = jnp.pad(extra, ((0, 0), (0, -extra.shape[1] % 128)))
    first = jnp.concatenate([ffn_in[:, :half], extra], axis=1)
    second = ffn_in[:, half:]

    def along_x(values):
        return swap(values, "exp", n_exp, 2)

    def along_y(values):
        return swap(values, "seq", n_seq, 1)

    total = 0.0
    for far in range(n_seq // 2):
        a0 = first if far == 0 else swap(first, "seq", n_seq, 2 * far)
        b0 = second if far == 0 else swap(second, "seq", n_seq, 2 * far)
        ax, ay, bx, by = along_x(a0), along_y(a0), along_x(b0), along_y(b0)
        axy, bxy = along_y(ax), along_x(by)
        left = jnp.concatenate([a0, ax, ay, axy], axis=0)
        right = jnp.concatenate([b0, bx, by, bxy], axis=0)
        tokens = jnp.concatenate([left[:, :half], right], axis=1)
        table = left[:, half:].astype(jnp.float32)
        lanes = jnp.arange(table.shape[1], dtype=jnp.int32)[None, :]
        partial = 0.0
        for m in range(2):
            mine = (lanes == ids[m]) | (lanes == ids[m] + experts)
            gate = jnp.sum(jnp.where(mine, table, 0.0), axis=1, keepdims=True)
            both = jnp.dot(tokens, in_weights[m], preferred_element_type=jnp.float32)
            act = (jax.nn.silu(both[:, :width]) * both[:, width:] * gate).astype(jnp.bfloat16)
            partial = partial + jnp.dot(act, out_weights[m], preferred_element_type=jnp.float32)
        partial = partial.astype(jnp.bfloat16)

        def added(kept, sent, along):
            return (kept.astype(jnp.float32) + along(sent).astype(jnp.float32)).astype(
                jnp.bfloat16
            )

        pa = partial[:, :half]
        pb = partial[:, half:]
        pa = added(pa[: 2 * rows], pa[2 * rows :], along_y)
        pa = added(pa[:rows], pa[rows:], along_x)
        near = jnp.concatenate([pb[:rows], pb[2 * rows : 3 * rows]], axis=0)
        away = jnp.concatenate([pb[rows : 2 * rows], pb[3 * rows :]], axis=0)
        pb = added(near, away, along_x)
        pb = added(pb[:rows], pb[rows:], along_y)
        if far > 0:
            pa = swap(pa, "seq", n_seq, 2 * far)
            pb = swap(pb, "seq", n_seq, 2 * far)
        total = total + jnp.concatenate([pa, pb], axis=1).astype(jnp.float32)
    return total


def experts_exchanged(ffn_in, router_weight, routes, expert_in, expert_out):
    tok_count = ffn_in.shape[0]
    experts = router_weight.shape[1]
    capacity = 2 * tok_count * TOPK // experts
    probs, chosen = router_gates(ffn_in, router_weight, routes)
    picked = jnp.sum(jnp.where(chosen, probs[:, None, :], 0.0), axis=-1)
    gates = picked / jnp.sum(picked, axis=-1, keepdims=True)
    flat_hot = chosen.reshape(tok_count * TOPK, experts).astype(jnp.int32)
    before = jnp.cumsum(flat_hot, axis=0) - flat_hot
    slots = jnp.sum(before * flat_hot, axis=-1).reshape(tok_count, TOPK)
    slot_hot = slots[:, :, None] == jnp.arange(capacity, dtype=jnp.int32)[None, None, :]
    placing = jnp.sum(
        (chosen[:, :, :, None] & slot_hot[:, :, None, :]).astype(jnp.bfloat16), axis=1
    )
    sending = jnp.einsum("tec,td->ecd", placing, ffn_in, preferred_element_type=jnp.float32).astype(
        jnp.bfloat16
    )
    received = lax.all_to_all(sending, ("exp", "seq"), split_axis=0, concat_axis=0, tiled=True)
    flat = received.reshape(-1, received.shape[-1])
    both = jnp.dot(flat, expert_in[0], preferred_element_type=jnp.float32)
    width = expert_out.shape[1]
    act = (jax.nn.silu(both[:, :width]) * both[:, width:]).astype(jnp.bfloat16)
    result = jnp.dot(act, expert_out[0], preferred_element_type=jnp.float32).astype(jnp.bfloat16)
    returned = lax.all_to_all(
        result.reshape(received.shape), ("exp", "seq"), split_axis=0, concat_axis=0, tiled=True
    )
    index = (routes * capacity + slots).reshape(-1)
    rows = jnp.take(returned.reshape(experts * capacity, -1), index, axis=0).reshape(
        tok_count, TOPK, -1
    )
    mixture = jnp.einsum("tk,tkd->td", gates, rows.astype(jnp.float32))
    return mixture


def local(
    hidden_in,
    doc_ids,
    attn_gain,
    q_weight,
    kv_weight,
    q_gain,
    k_gain,
    out_weight,
    ffn_gain,
    router_weight,
    routes,
    expert_in,
    expert_out,
    *,
    n_exp,
    n_seq,
):
    attn_rows = attention_rows(
        hidden_in, doc_ids, attn_gain, q_weight, kv_weight, q_gain, k_gain, out_weight, n_exp, n_seq
    )
    mid = (hidden_in.astype(jnp.float32) + attn_rows).astype(jnp.bfloat16)
    ffn_in = rms_scale(mid.astype(jnp.float32), ffn_gain).astype(jnp.bfloat16)
    tok_count = hidden_in.shape[0]
    capacity = 2 * tok_count * TOPK // router_weight.shape[1]
    if n_exp == 4 and 2 * capacity >= tok_count:
        mixture = experts_gathered(
            ffn_in, router_weight, routes, expert_in, expert_out, n_exp, n_seq
        )
    else:
        mixture = experts_exchanged(ffn_in, router_weight, routes, expert_in, expert_out)
    return (mid.astype(jnp.float32) + mixture).astype(jnp.bfloat16)


def solution(mesh):
    in_specs = (
        P(("exp", "seq"), None),
        P(("exp", "seq")),
        P(),
        P("exp", "seq"),
        P(None, "exp", None),
        P(),
        P(),
        P("seq", "exp"),
        P(),
        P(),
        P(("exp", "seq"), None),
        P(("exp", "seq"), None, None),
        P(("exp", "seq"), None, None),
    )
    out_specs = P(("exp", "seq"), None)
    body = functools.partial(local, n_exp=mesh.shape["exp"], n_seq=mesh.shape["seq"])
    return jax.shard_map(body, mesh=mesh, in_specs=in_specs, out_specs=out_specs, check_vma=False)
```

time: 710 us -> 574 us (0.81); the launches traced: 710 us -> 566 us
  blocking collectives: 202 us -> 11.9 us
  waiting for transfers between devices: 411 us -> 260 us
  starting transfers between devices: 4.23 us -> 92.6 us
  matrix products: 48.8 us -> 133 us
  local copies, waits for them, and re-layouts: 17 us -> 38.3 us
  other arithmetic: 13.3 us -> 28.3 us
  between operations: 14.1 us -> 2.71 us
    ppermute x0 -> x74, waiting for transfers between devices: none -> 260 us  [swap(): return lax.ppermute(values, axis, [(i, i ^ mask) for i in range(size)])]
    all_to_all x1 -> x0, blocking collectives: 189 us -> none  [local(): lax.all_to_all(sending, ('exp', 'seq'), split_axis=0, concat_axis=0, tile...]
    all_to_all x1 -> x0, waiting for transfers between devices: 188 us -> none  [local(): lax.all_to_all(result.reshape(received.shape), ('exp', 'seq'), split_axis...]
    all_gather x4 -> x0, waiting for transfers between devices: 136 us -> none  [the longest x1 75 us: local(): lax.all_gather(normed, 'seq', axis=0, tiled=True)]
    ppermute x0 -> x74, starting transfers between devices: none -> 92.6 us  [swap(): return lax.ppermute(values, axis, [(i, i ^ mask) for i in range(size)])]
    reduce_scatter x1 -> x0, waiting for transfers between devices: 85.1 us -> none  [local(): lax.psum_scatter(jnp.dot(context, out_full, preferred_element_type=jnp.fl...]
    dot_general x10 -> x33, matrix products: 48.8 us -> 129 us  [the longest x8 54.3 us: experts_gathered(): both = jnp.dot(tokens, in_weights[m], preferred_element_type=jnp.float32)]
    rev x0 -> x4, local copies, waits for them, and re-layouts: none -> 14.9 us  [permute_blocks(): parts = jnp.where(own & bit != 0, parts[..., ::-1, :], parts)]
  transfers between devices with their start and end apart: 6 -> 74, of which waited for: 6 -> 34; matrix products, arithmetic and copies ran while one was open for 4% -> 24% of each run, Pallas kernels for 0% -> 0%
where the time goes in v1:
time: 574 us; the launch traced here: 566 us
  waiting for transfers between devices  260 us (45%)
  matrix products  133 us (23%)
  starting transfers between devices  92.6 us (16%)
  local copies, waits for them, and re-layouts  38.3 us (7%)
  other arithmetic  28.3 us (5%)
  blocking collectives  11.9 us (2%)
    ppermute x74, waiting for transfers between devices, swap(): return lax.ppermute(values, axis, [(i, i ^ mask) for i in range(size)])  260 us
    ppermute x74, starting transfers between devices, swap(): return lax.ppermute(values, axis, [(i, i ^ mask) for i in range(size)])  92.6 us
    dot_general x8, matrix products, experts_gathered(): both = jnp.dot(tokens, in_weights[m], preferred_element_type=jnp.float32)  54.3 us
    dot_general x8, matrix products, experts_gathered(): jnp.dot(act, out_weights[m], preferred_element_type=jnp.float32)  41.4 us
    rev x4, local copies, waits for them, and re-layouts, permute_blocks(): parts = jnp.where(own & bit != 0, parts[..., ::-1, :], parts)  14.9 us
    dot_general x4, matrix products, attention_rows(): jnp.dot(context, out_full, preferred_element_type=jnp.float32)  12.1 us
    unnamed x1, blocking collectives  11.9 us
  transfers between devices with their start and end apart: 74, of which 34 were waited for; matrix products, arithmetic and copies ran while one was open for 24% of the time, Pallas kernels for 0%

profile of v1, /device:TPU:0, one launch (start us, length us, event | category | flops | bytes accessed | tf_op | source)
XLA Modules:
  0.0 566.4 jit_solution(13827737510253172404)
XLA Ops:
  17.4 46.9 %collective-permute-done.11 = bf16[512,1024]{1,0:T(8,128)(2,1)} collective-permute-done((bf16[512,1024]{1,0:T(8,128)(2,1)}, bf16[512,1024]{1,0:T(8,128)(2,1)}, u32[]{:S(2)}, u32[]{:S(2)}) %collective-permute-start.11) | collective-permute-done | bytes 1048608 | tf_op jit(solution)/shard_map/ppermute | solution.py:35
  66.2 11.9 %all-reduce.1 = s32[512]{0:T(512)S(1)} all-reduce(s32[512]{0:T(512)S(1)} %dynamic-update-slice), channel_id=2, replica_groups=mesh['exp'=4,'seq'=8] {'seq'}, use_global_device_ids=true, to_apply=%add.1 | all-reduce | flops 512 | bytes 4096
  91.8 27.9 %collective-permute-done.6 = bf16[64,4096]{1,0:T(8,128)(2,1)S(1)} collective-permute-done((bf16[64,4096]{1,0:T(8,128)(2,1)S(1)}, bf16[64,4096]{1,0:T(8,128)(2,1)S(1)}, u32[]{:S(2)}, u32[]{:S(2)}) %collective-permute-start.6) | collective-permute-done | bytes 524320 | tf_op jit(solution)/shard_map/ppermute | solution.py:35
  123.2 8.0 %pad_maximum_fusion = bf16[4096,768]{1,0:T(8,128)(2,1)S(1)} fusion(bf16[1024,768]{1,0:T(8,128)(2,1)} %collective-permute-done.3, bf16[1024,768]{1,0:T(8,128)(2,1)} %collective-permute-done.2, bf16[1024,768]{1,0:T(8,128)(2,1)} %collective-permute-done.1, bf16[1024,256]{1,0:T(8,128)(2,1)S(1)} %dynamic-slice_bitcast_fusion, bf16[1024,512]{1,0:T(8,128)(2,1)S(1)} %copy-done.6), kind=kLoop, calls=%fused_computation.5 | loop fusion | flops 31457280 | bytes 12582912 | tf_op jit(solution)/shard_map/concatenate | solution.py:88
  132.2 13.7 %collective-permute-done.7 = bf16[64,4096]{1,0:T(8,128)(2,1)S(1)} collective-permute-done((bf16[64,4096]{1,0:T(8,128)(2,1)S(1)}, bf16[64,4096]{1,0:T(8,128)(2,1)S(1)}, u32[]{:S(2)}, u32[]{:S(2)}) %collective-permute-start.7) | collective-permute-done | bytes 524320 | tf_op jit(solution)/shard_map/ppermute | solution.py:35
  146.9 9.3 %collective-permute-done.9 = bf16[64,4096]{1,0:T(8,128)(2,1)S(1)} collective-permute-done((bf16[64,4096]{1,0:T(8,128)(2,1)S(1)}, bf16[64,4096]{1,0:T(8,128)(2,1)S(1)}, u32[]{:S(2)}, u32[]{:S(2)}) %collective-permute-start.9) | collective-permute-done | bytes 524320 | tf_op jit(solution)/shard_map/ppermute | solution.py:35
  190.5 3.1 convolution_convert_fusion.2
  209.5 3.8 collective-permute-done.15
  214.5 9.9 %collective-permute-done.17 = bf16[64,4096]{1,0:T(8,128)(2,1)S(1)} collective-permute-done((bf16[64,4096]{1,0:T(8,128)(2,1)}, bf16[64,4096]{1,0:T(8,128)(2,1)S(1)}, u32[]{:S(2)}, u32[]{:S(2)}) %collective-permute-start.17) | collective-permute-done | bytes 524320 | tf_op jit(solution)/shard_map/ppermute | solution.py:35
  225.0 8.9 %collective-permute-done.19 = bf16[64,4096]{1,0:T(8,128)(2,1)S(1)} collective-permute-done((bf16[64,4096]{1,0:T(8,128)(2,1)S(1)}, bf16[64,4096]{1,0:T(8,128)(2,1)S(1)}, u32[]{:S(2)}, u32[]{:S(2)}) %collective-permute-start.19) | collective-permute-done | bytes 524320 | tf_op jit(solution)/shard_map/ppermute | solution.py:35
  233.8 21.0 %collective-permute-done.16 = bf16[64,4096]{1,0:T(8,128)(2,1)S(1)} collective-permute-done((bf16[64,4096]{1,0:T(8,128)(2,1)S(1)}, bf16[64,4096]{1,0:T(8,128)(2,1)S(1)}, u32[]{:S(2)}, u32[]{:S(2)}) %collective-permute-start.16) | collective-permute-done | bytes 524320 | tf_op jit(solution)/shard_map/ppermute | solution.py:35
  256.1 6.5 %rev.14 = f32[64,1,2,2048]{3,2,0,1:T(2,128)} reverse(f32[64,1,2,2048]{3,2,0,1:T(2,128)S(1)} %reshape.901), dimensions={2} | reverse | bytes 2097152 | tf_op jit(solution)/shard_map/rev | solution.py:44
  273.1 3.2 collective-permute-start.46
  276.3 6.9 %collective-permute-done.60 = bf16[64,2176]{1,0:T(8,128)(2,1)S(1)} collective-permute-done((bf16[64,2176]{1,0:T(8,128)(2,1)S(1)}, bf16[64,2176]{1,0:T(8,128)(2,1)S(1)}, u32[]{:S(2)}, u32[]{:S(2)}) %collective-permute-start.60) | collective-permute-done | bytes 278560 | tf_op jit(solution)/shard_map/ppermute | solution.py:35
  285.9 3.5 collective-permute-done.32
  290.9 4.1 collective-permute-done.46
  297.1 7.5 %collective-permute-done.24 = bf16[64,2048]{1,0:T(8,128)(2,1)S(1)} collective-permute-done((bf16[64,2048]{1,0:T(8,128)(2,1)S(1)}, bf16[64,2048]{1,0:T(8,128)(2,1)S(1)}, u32[]{:S(2)}, u32[]{:S(2)}) %collective-permute-start.24) | collective-permute-done | bytes 262176 | tf_op jit(solution)/shard_map/ppermute | solution.py:35
  313.0 8.6 %collective-permute-start.50 = (bf16[64,2048]{1,0:T(8,128)(2,1)S(1)}, bf16[64,2048]{1,0:T(8,128)(2,1)S(1)}, u32[]{:S(2)}, u32[]{:S(2)}) collective-permute-start(bf16[64,2048]{1,0:T(8,128)(2,1)S(1)} %get-tuple-element.38), channel_id=1, source_target_pairs={{0,4},{1,5},{2,6},{3,7},{4,0},{5,1},{6,2},{7,3},{8,12},{9,13},{10,... | collective-permute-start | bytes 786440 | tf_op jit(solution)/shard_map/ppermute | solution.py:35
  323.1 3.9 collective-permute-start.61
  327.0 9.2 %fusion.191 = f32[256,1536]{1,0:T(8,128)} fusion(bf16[1,4096,1536]{2,1,0:T(8,128)(2,1)} %param.24, bf16[64,2048]{1,0:T(8,128)(2,1)S(1)} %collective-permute-done.25, bf16[64,2048]{1,0:T(8,128)(2,1)S(1)} %collective-permute-done.24, bf16[64,2048]{1,0:T(8,128)(2,1)S(1)} %collective-permute-done.23, bf16[64,2048]{1,0:T(8,128)(2,1)S(1)} %get-tuple-element.38, ...), kind=kOutput, calls=%fused_computation.348 | convolution fusion | flops 3231711232 | bytes 16252928 | tf_op jit(solution)/shard_map/dot_general | solution.py:180
  336.8 6.5 %collective-permute-done.62 = bf16[64,2176]{1,0:T(8,128)(2,1)S(1)} collective-permute-done((bf16[64,2176]{1,0:T(8,128)(2,1)S(1)}, bf16[64,2176]{1,0:T(8,128)(2,1)S(1)}, u32[]{:S(2)}, u32[]{:S(2)}) %collective-permute-start.62) | collective-permute-done | bytes 278560 | tf_op jit(solution)/shard_map/ppermute | solution.py:35
  343.3 8.1 %collective-permute-done.33 = bf16[64,2176]{1,0:T(8,128)(2,1)S(1)} collective-permute-done((bf16[64,2176]{1,0:T(8,128)(2,1)S(1)}, bf16[64,2176]{1,0:T(8,128)(2,1)S(1)}, u32[]{:S(2)}, u32[]{:S(2)}) %collective-permute-start.33) | collective-permute-done | bytes 278560 | tf_op jit(solution)/shard_map/ppermute | solution.py:35
  351.5 9.3 %collective-permute-done.34 = bf16[64,2176]{1,0:T(8,128)(2,1)S(1)} collective-permute-done((bf16[64,2176]{1,0:T(8,128)(2,1)S(1)}, bf16[64,2176]{1,0:T(8,128)(2,1)S(1)}, u32[]{:S(2)}, u32[]{:S(2)}) %collective-permute-start.34) | collective-permute-done | bytes 278560 | tf_op jit(solution)/shard_map/ppermute | solution.py:35
  360.8 8.8 %collective-permute-done.47 = bf16[64,2176]{1,0:T(8,128)(2,1)S(1)} collective-permute-done((bf16[64,2176]{1,0:T(8,128)(2,1)S(1)}, bf16[64,2176]{1,0:T(8,128)(2,1)S(1)}, u32[]{:S(2)}, u32[]{:S(2)}) %collective-permute-start.47) | collective-permute-done | bytes 278560 | tf_op jit(solution)/shard_map/ppermute | solution.py:35
  369.6 9.5 %collective-permute-done.48 = bf16[64,2176]{1,0:T(8,128)(2,1)S(1)} collective-permute-done((bf16[64,2176]{1,0:T(8,128)(2,1)S(1)}, bf16[64,2176]{1,0:T(8,128)(2,1)S(1)}, u32[]{:S(2)}, u32[]{:S(2)}) %collective-permute-start.48) | collective-permute-done | bytes 278560 | tf_op jit(solution)/shard_map/ppermute | solution.py:35
  379.5 9.1 %collective-permute-done.63 = bf16[64,2176]{1,0:T(8,128)(2,1)S(1)} collective-permute-done((bf16[64,2176]{1,0:T(8,128)(2,1)S(1)}, bf16[64,2176]{1,0:T(8,128)(2,1)S(1)}, u32[]{:S(2)}, u32[]{:S(2)}) %collective-permute-start.63) | collective-permute-done | bytes 278560 | tf_op jit(solution)/shard_map/ppermute | solution.py:35
  389.8 6.5 %collective-permute-done.67 = bf16[64,2048]{1,0:T(8,128)(2,1)S(1)} collective-permute-done((bf16[64,2048]{1,0:T(8,128)(2,1)S(1)}, bf16[64,2048]{1,0:T(8,128)(2,1)S(1)}, u32[]{:S(2)}, u32[]{:S(2)}) %collective-permute-start.67) | collective-permute-done | bytes 262176 | tf_op jit(solution)/shard_map/ppermute | solution.py:35
  397.0 4.6 fusion.185
  405.9 3.6 collective-permute-done.49
  410.5 5.2 fusion.73
  418.0 5.0 fusion.187
  423.0 7.2 %fusion.70 = f32[256,4096]{1,0:T(8,128)} fusion(f32[256,1536]{1,0:T(8,128)} %fusion.187, f32[256]{0:T(256)S(1)} %get-tuple-element.15, bf16[1,768,4096]{2,1,0:T(8,128)(2,1)} %param.25), kind=kOutput, calls=%fused_computation.137 | convolution fusion | flops 1611988992 | bytes 12059648 | tf_op jit(solution)/shard_map/dot_general | solution.py:182
  430.4 3.4 fusion.189
  433.8 4.8 fusion.67
  438.7 4.7 fusion.64
  443.4 8.0 %fusion.210 = f32[256,1536]{1,0:T(8,128)S(1)} fusion(bf16[4096,1536]{1,0:T(8,128)(2,1)} %collective-permute-done.26, bf16[64,2048]{1,0:T(8,128)(2,1)S(1)} %collective-permute-done.67, bf16[64,2048]{1,0:T(8,128)(2,1)S(1)} %collective-permute-done.66, bf16[64,2048]{1,0:T(8,128)(2,1)S(1)} %collective-permute-done.65, ...), kind=kOutput, calls=%fused_computation.371 | convolution fusion | flops 3231711232 | bytes 16252928 | tf_op jit(solution)/shard_map/dot_general | solution.py:180
  451.4 4.9 fusion.7
  456.6 8.1 %fusion.211 = f32[256,1536]{1,0:T(8,128)S(1)} fusion(bf16[4096,1536]{1,0:T(8,128)(2,1)} %collective-permute-done.26, bf16[64,2048]{1,0:T(8,128)(2,1)S(1)} %collective-permute-done.53, bf16[64,2048]{1,0:T(8,128)(2,1)S(1)} %collective-permute-done.52, bf16[64,2048]{1,0:T(8,128)(2,1)S(1)} %collective-permute-done.51, ...), kind=kOutput, calls=%fused_computation.372 | convolution fusion | flops 3231711232 | bytes 16252928 | tf_op jit(solution)/shard_map/dot_general | solution.py:180
  464.8 4.8 fusion.6
  469.8 8.0 %fusion.212 = f32[256,1536]{1,0:T(8,128)S(1)} fusion(bf16[4096,1536]{1,0:T(8,128)(2,1)} %collective-permute-done.26, bf16[64,2048]{1,0:T(8,128)(2,1)S(1)} %collective-permute-done.39, bf16[64,2048]{1,0:T(8,128)(2,1)S(1)} %collective-permute-done.38, bf16[64,2048]{1,0:T(8,128)(2,1)S(1)} %collective-permute-done.37, ...), kind=kOutput, calls=%fused_computation.373 | convolution fusion | flops 3231711232 | bytes 16252928 | tf_op jit(solution)/shard_map/dot_general | solution.py:180
  477.8 4.8 fusion.5
  486.8 8.0 %fusion.213 = f32[256,1536]{1,0:T(8,128)S(1)} fusion(bf16[4096,1536]{1,0:T(8,128)(2,1)} %collective-permute-done.26, bf16[64,2048]{1,0:T(8,128)(2,1)S(1)} %collective-permute-done.25, bf16[64,2048]{1,0:T(8,128)(2,1)S(1)} %collective-permute-done.24, bf16[64,2048]{1,0:T(8,128)(2,1)S(1)} %collective-permute-done.23, ...), kind=kOutput, calls=%fused_computation.374 | convolution fusion | flops 3231711232 | bytes 16252928 | tf_op jit(solution)/shard_map/dot_general | solution.py:180
  494.8 4.8 fusion.4
  505.2 4.6 collective-permute-done.40
  510.4 4.5 collective-permute-done.71
  517.4 6.9 %collective-permute-done.43 = bf16[128,2048]{1,0:T(8,128)(2,1)S(1)} collective-permute-done((bf16[128,2048]{1,0:T(8,128)(2,1)S(1)}, bf16[128,2048]{1,0:T(8,128)(2,1)S(1)}, u32[]{:S(2)}, u32[]{:S(2)}) %collective-permute-start.43) | collective-permute-done | bytes 524320 | tf_op jit(solution)/shard_map/ppermute | solution.py:35
  545.3 9.8 %collective-permute-start.45 = (bf16[64,2048]{1,0:T(8,128)(2,1)S(1)}, bf16[64,2048]{1,0:T(8,128)(2,1)S(1)}, u32[]{:S(2)}, u32[]{:S(2)}) collective-permute-start(bf16[64,2048]{1,0:T(8,128)(2,1)S(1)} %add_convert_fusion.15), channel_id=1, source_target_pairs={{0,2},{1,3},{2,0},{3,1},{4,6},{5,7},{6,4},{7,5},{8,10},{9,11},{10,... | collective-permute-start | bytes 786440 | tf_op jit(solution)/shard_map/ppermute | solution.py:35
  555.2 5.1 collective-permute-done.56
  (427 shorter events, 167.4 us)
Async XLA Ops:
  4.2 74.6 %collective-permute-start.2 = (bf16[1024,768]{1,0:T(8,128)(2,1)}, bf16[1024,768]{1,0:T(8,128)(2,1)}, u32[]{:S(2)}, u32[]{:S(2)}) collective-permute-start(bf16[1024,768]{1,0:T(8,128)(2,1)} %pad_maximum_fusion.1), channel_id=1, source_target_pairs={{0,16},{8,24},{16,0},{24,8},{1,17},{9,25},{17,1},{25,9},{2,18},{10... | collective-permute-start | bytes 4718600 | tf_op jit(solution)/shard_map/ppermute | solution.py:35
  7.1 114.6 %collective-permute-start.1 = (bf16[1024,768]{1,0:T(8,128)(2,1)}, bf16[1024,768]{1,0:T(8,128)(2,1)}, u32[]{:S(2)}, u32[]{:S(2)}) collective-permute-start(bf16[1024,768]{1,0:T(8,128)(2,1)} %pad_maximum_fusion.1), channel_id=1, source_target_pairs={{0,8},{8,0},{16,24},{24,16},{1,9},{9,1},{17,25},{25,17},{2,10},{10... | collective-permute-start | bytes 4718600 | tf_op jit(solution)/shard_map/ppermute | solution.py:35
  7.1 57.2 %collective-permute-start.11 = (bf16[512,1024]{1,0:T(8,128)(2,1)}, bf16[512,1024]{1,0:T(8,128)(2,1)}, u32[]{:S(2)}, u32[]{:S(2)}) collective-permute-start(bf16[512,1024]{1,0:T(8,128)(2,1)} %param.20), channel_id=1, source_target_pairs={{0,16},{8,24},{16,0},{24,8},{1,17},{9,25},{17,1},{25,9},{2,18},{10... | collective-permute-start | bytes 3145736 | tf_op jit(solution)/shard_map/ppermute | solution.py:35
  7.2 74.8 %collective-permute-start.10 = (bf16[512,1024]{1,0:T(8,128)(2,1)}, bf16[512,1024]{1,0:T(8,128)(2,1)}, u32[]{:S(2)}, u32[]{:S(2)}) collective-permute-start(bf16[512,1024]{1,0:T(8,128)(2,1)} %param.20), channel_id=1, source_target_pairs={{0,8},{8,0},{16,24},{24,16},{1,9},{9,1},{17,25},{25,17},{2,10},{10... | collective-permute-start | bytes 3145736 | tf_op jit(solution)/shard_map/ppermute | solution.py:35
  15.4 74.7 %collective-permute-start.4 = (bf16[64,4096]{1,0:T(8,128)(2,1)S(1)}, bf16[64,4096]{1,0:T(8,128)(2,1)}, u32[]{:S(2)}, u32[]{:S(2)}) collective-permute-start(bf16[64,4096]{1,0:T(8,128)(2,1)S(1)} %reshape.892), channel_id=1, source_target_pairs={{0,2},{1,3},{2,0},{3,1},{4,6},{5,7},{6,4},{7,5},{8,10},{9,11},{10,... | collective-permute-start | bytes 1572872 | tf_op jit(solution)/shard_map/ppermute | solution.py:35
  64.3 18.1 %collective-permute-start.12 = (bf16[512,1024]{1,0:T(8,128)(2,1)}, bf16[512,1024]{1,0:T(8,128)(2,1)}, u32[]{:S(2)}, u32[]{:S(2)}) collective-permute-start(bf16[512,1024]{1,0:T(8,128)(2,1)} %collective-permute-done.11), channel_id=1, source_target_pairs={{0,8},{8,0},{16,24},{24,16},{1,9},{9,1},{17,25},{25,17},{2,10},{10... | collective-permute-start | bytes 3145736 | tf_op jit(solution)/shard_map/ppermute | solution.py:35
  78.7 44.5 %collective-permute-start.3 = (bf16[1024,768]{1,0:T(8,128)(2,1)}, bf16[1024,768]{1,0:T(8,128)(2,1)}, u32[]{:S(2)}, u32[]{:S(2)}) collective-permute-start(bf16[1024,768]{1,0:T(8,128)(2,1)} %collective-permute-done.2), channel_id=1, source_target_pairs={{0,8},{8,0},{16,24},{24,16},{1,9},{9,1},{17,25},{25,17},{2,10},{10... | collective-permute-start | bytes 4718600 | tf_op jit(solution)/shard_map/ppermute | solution.py:35
  82.0 37.7 %collective-permute-start.6 = (bf16[64,4096]{1,0:T(8,128)(2,1)S(1)}, bf16[64,4096]{1,0:T(8,128)(2,1)S(1)}, u32[]{:S(2)}, u32[]{:S(2)}) collective-permute-start(bf16[64,4096]{1,0:T(8,128)(2,1)S(1)} %reshape.892), channel_id=1, source_target_pairs={{0,4},{1,5},{2,6},{3,7},{4,0},{5,1},{6,2},{7,3},{8,12},{9,13},{10,... | collective-permute-start | bytes 1572872 | tf_op jit(solution)/shard_map/ppermute | solution.py:35
  82.4 38.8 %collective-permute-start.8 = (bf16[64,4096]{1,0:T(8,128)(2,1)S(1)}, bf16[64,4096]{1,0:T(8,128)(2,1)S(1)}, u32[]{:S(2)}, u32[]{:S(2)}) collective-permute-start(bf16[64,4096]{1,0:T(8,128)(2,1)S(1)} %reshape.892), channel_id=1, source_target_pairs={{0,6},{1,7},{2,4},{3,5},{4,2},{5,3},{6,0},{7,1},{8,14},{9,15},{10,... | collective-permute-start | bytes 1572872 | tf_op jit(solution)/shard_map/ppermute | solution.py:35
  90.2 41.0 %collective-permute-start = (bf16[64,4096]{1,0:T(8,128)(2,1)S(1)}, bf16[64,4096]{1,0:T(8,128)(2,1)S(1)}, u32[]{:S(2)}, u32[]{:S(2)}) collective-permute-start(bf16[64,4096]{1,0:T(8,128)(2,1)S(1)} %reshape.892), channel_id=1, source_target_pairs={{0,1},{1,0},{2,3},{3,2},{4,5},{5,4},{6,7},{7,6},{8,9},{9,8},{10,11... | collective-permute-start | bytes 1572872 | tf_op jit(solution)/shard_map/ppermute | solution.py:35
  119.7 39.2 %collective-permute-start.5 = (bf16[64,4096]{1,0:T(8,128)(2,1)}, bf16[64,4096]{1,0:T(8,128)(2,1)S(1)}, u32[]{:S(2)}, u32[]{:S(2)}) collective-permute-start(bf16[64,4096]{1,0:T(8,128)(2,1)} %collective-permute-done.4), channel_id=1, source_target_pairs={{0,1},{1,0},{2,3},{3,2},{4,5},{5,4},{6,7},{7,6},{8,9},{9,8},{10,11... | collective-permute-start | bytes 1572872 | tf_op jit(solution)/shard_map/ppermute | solution.py:35
  121.2 24.7 %collective-permute-start.7 = (bf16[64,4096]{1,0:T(8,128)(2,1)S(1)}, bf16[64,4096]{1,0:T(8,128)(2,1)S(1)}, u32[]{:S(2)}, u32[]{:S(2)}) collective-permute-start(bf16[64,4096]{1,0:T(8,128)(2,1)S(1)} %collective-permute-done.6), channel_id=1, source_target_pairs={{0,1},{1,0},{2,3},{3,2},{4,5},{5,4},{6,7},{7,6},{8,9},{9,8},{10,11... | collective-permute-start | bytes 1572872 | tf_op jit(solution)/shard_map/ppermute | solution.py:35
  121.7 34.5 %collective-permute-start.9 = (bf16[64,4096]{1,0:T(8,128)(2,1)S(1)}, bf16[64,4096]{1,0:T(8,128)(2,1)S(1)}, u32[]{:S(2)}, u32[]{:S(2)}) collective-permute-start(bf16[64,4096]{1,0:T(8,128)(2,1)S(1)} %collective-permute-done.8), channel_id=1, source_target_pairs={{0,1},{1,0},{2,3},{3,2},{4,5},{5,4},{6,7},{7,6},{8,9},{9,8},{10,11... | collective-permute-start | bytes 1572872 | tf_op jit(solution)/shard_map/ppermute | solution.py:35
  186.9 21.3 %collective-permute-start.13 = (bf16[64,4096]{1,0:T(8,128)(2,1)}, bf16[64,4096]{1,0:T(8,128)(2,1)}, u32[]{:S(2)}, u32[]{:S(2)}) collective-permute-start(bf16[64,4096]{1,0:T(8,128)(2,1)} %slice.526), channel_id=1, source_target_pairs={{0,1},{1,0},{2,3},{3,2},{4,5},{5,4},{6,7},{7,6},{8,9},{9,8},{10,11... | collective-permute-start | bytes 1572872 | tf_op jit(solution)/shard_map/ppermute | solution.py:35
  194.5 18.7 %collective-permute-start.15 = (bf16[64,4096]{1,0:T(8,128)(2,1)}, bf16[64,4096]{1,0:T(8,128)(2,1)}, u32[]{:S(2)}, u32[]{:S(2)}) collective-permute-start(bf16[64,4096]{1,0:T(8,128)(2,1)} %slice.531), channel_id=1, source_target_pairs={{0,1},{1,0},{2,3},{3,2},{4,5},{5,4},{6,7},{7,6},{8,9},{9,8},{10,11... | collective-permute-start | bytes 1572872 | tf_op jit(solution)/shard_map/ppermute | solution.py:35
  200.9 23.5 %collective-permute-start.17 = (bf16[64,4096]{1,0:T(8,128)(2,1)}, bf16[64,4096]{1,0:T(8,128)(2,1)S(1)}, u32[]{:S(2)}, u32[]{:S(2)}) collective-permute-start(bf16[64,4096]{1,0:T(8,128)(2,1)} %slice.536), channel_id=1, source_target_pairs={{0,1},{1,0},{2,3},{3,2},{4,5},{5,4},{6,7},{7,6},{8,9},{9,8},{10,11... | collective-permute-start | bytes 1572872 | tf_op jit(solution)/shard_map/ppermute | solution.py:35
  207.6 26.2 %collective-permute-start.19 = (bf16[64,4096]{1,0:T(8,128)(2,1)S(1)}, bf16[64,4096]{1,0:T(8,128)(2,1)S(1)}, u32[]{:S(2)}, u32[]{:S(2)}) collective-permute-start(bf16[64,4096]{1,0:T(8,128)(2,1)S(1)} %slice.541), channel_id=1, source_target_pairs={{0,1},{1,0},{2,3},{3,2},{4,5},{5,4},{6,7},{7,6},{8,9},{9,8},{10,11... | collective-permute-start | bytes 1572872 | tf_op jit(solution)/shard_map/ppermute | solution.py:35
  209.4 24.5 %collective-permute-start.14 = (bf16[64,4096]{1,0:T(8,128)(2,1)S(1)}, bf16[64,4096]{1,0:T(8,128)(2,1)S(1)}, u32[]{:S(2)}, u32[]{:S(2)}) collective-permute-start(bf16[64,4096]{1,0:T(8,128)(2,1)S(1)} %add_convert_fusion.10), channel_id=1, source_target_pairs={{0,6},{1,7},{2,4},{3,5},{4,2},{5,3},{6,0},{7,1},{8,14},{9,15},{10,... | collective-permute-start | bytes 1572872 | tf_op jit(solution)/shard_map/ppermute | solution.py:35
  214.4 40.4 %collective-permute-start.16 = (bf16[64,4096]{1,0:T(8,128)(2,1)S(1)}, bf16[64,4096]{1,0:T(8,128)(2,1)S(1)}, u32[]{:S(2)}, u32[]{:S(2)}) collective-permute-start(bf16[64,4096]{1,0:T(8,128)(2,1)S(1)} %add_convert_fusion.9), channel_id=1, source_target_pairs={{0,4},{1,5},{2,6},{3,7},{4,0},{5,1},{6,2},{7,3},{8,12},{9,13},{10,... | collective-permute-start | bytes 1572872 | tf_op jit(solution)/shard_map/ppermute | solution.py:35
  224.5 30.3 %collective-permute-start.18 = (bf16[64,4096]{1,0:T(8,128)(2,1)S(1)}, bf16[64,4096]{1,0:T(8,128)(2,1)S(1)}, u32[]{:S(2)}, u32[]{:S(2)}) collective-permute-start(bf16[64,4096]{1,0:T(8,128)(2,1)S(1)} %add_convert_fusion.8), channel_id=1, source_target_pairs={{0,2},{1,3},{2,0},{3,1},{4,6},{5,7},{6,4},{7,5},{8,10},{9,11},{10,... | collective-permute-start | bytes 1572872 | tf_op jit(solution)/shard_map/ppermute | solution.py:35
  224.9 218.5 %collective-permute-start.26 = (bf16[4096,1536]{1,0:T(8,128)(2,1)}, bf16[4096,1536]{1,0:T(8,128)(2,1)}, u32[]{:S(2)}, u32[]{:S(2)}) collective-permute-start(bf16[4096,1536]{1,0:T(8,128)(2,1)} %bitcast.187), channel_id=1, source_target_pairs={{0,8},{8,0},{16,24},{24,16},{1,9},{9,1},{17,25},{25,17},{2,10},{10... | collective-permute-start | bytes 37748744 | tf_op jit(solution)/shard_map/ppermute | solution.py:35
  273.0 178.4 %collective-permute-start.27 = (bf16[768,4096]{1,0:T(8,128)(2,1)}, bf16[768,4096]{1,0:T(8,128)(2,1)}, u32[]{:S(2)}, u32[]{:S(2)}) collective-permute-start(bf16[768,4096]{1,0:T(8,128)(2,1)} %bitcast.190), channel_id=1, source_target_pairs={{0,8},{8,0},{16,24},{24,16},{1,9},{9,1},{17,25},{25,17},{2,10},{10... | collective-permute-start | bytes 18874376 | tf_op jit(solution)/shard_map/ppermute | solution.py:35
  273.0 16.4 %collective-permute-start.32 = (bf16[64,2176]{1,0:T(8,128)(2,1)S(1)}, bf16[64,2176]{1,0:T(8,128)(2,1)S(1)}, u32[]{:S(2)}, u32[]{:S(2)}) collective-permute-start(bf16[64,2176]{1,0:T(8,128)(2,1)S(1)} %pad_maximum_fusion.7), channel_id=1, source_target_pairs={{0,2},{1,3},{2,0},{3,1},{4,6},{5,7},{6,4},{7,5},{8,10},{9,11},{10,... | collective-permute-start | bytes 835592 | tf_op jit(solution)/shard_map/ppermute | solution.py:35
  273.1 21.9 %collective-permute-start.46 = (bf16[64,2176]{1,0:T(8,128)(2,1)S(1)}, bf16[64,2176]{1,0:T(8,128)(2,1)S(1)}, u32[]{:S(2)}, u32[]{:S(2)}) collective-permute-start(bf16[64,2176]{1,0:T(8,128)(2,1)S(1)} %pad_maximum_fusion.7), channel_id=1, source_target_pairs={{0,4},{1,5},{2,6},{3,7},{4,0},{5,1},{6,2},{7,3},{8,12},{9,13},{10,... | collective-permute-start | bytes 835592 | tf_op jit(solution)/shard_map/ppermute | solution.py:35
  283.1 13.4 %collective-permute-start.20 = (bf16[64,2176]{1,0:T(8,128)(2,1)S(1)}, bf16[64,2176]{1,0:T(8,128)(2,1)S(1)}, u32[]{:S(2)}, u32[]{:S(2)}) collective-permute-start(bf16[64,2176]{1,0:T(8,128)(2,1)S(1)} %pad_maximum_fusion.7), channel_id=1, source_target_pairs={{0,16},{8,24},{16,0},{24,8},{1,17},{9,25},{17,1},{25,9},{2,18},{10... | collective-permute-start | bytes 835592 | tf_op jit(solution)/shard_map/ppermute | solution.py:35
  289.4 17.6 %collective-permute-start.21 = (bf16[64,2176]{1,0:T(8,128)(2,1)S(1)}, bf16[64,2176]{1,0:T(8,128)(2,1)S(1)}, u32[]{:S(2)}, u32[]{:S(2)}) collective-permute-start(bf16[64,2176]{1,0:T(8,128)(2,1)S(1)} %pad_maximum_fusion.7), channel_id=1, source_target_pairs={{0,1},{1,0},{2,3},{3,2},{4,5},{5,4},{6,7},{7,6},{8,9},{9,8},{10,11... | collective-permute-start | bytes 835592 | tf_op jit(solution)/shard_map/ppermute | solution.py:35
  307.0 14.5 %collective-permute-start.23 = (bf16[64,2048]{1,0:T(8,128)(2,1)S(1)}, bf16[64,2048]{1,0:T(8,128)(2,1)S(1)}, u32[]{:S(2)}, u32[]{:S(2)}) collective-permute-start(bf16[64,2048]{1,0:T(8,128)(2,1)S(1)} %get-tuple-element.38), channel_id=1, source_target_pairs={{0,16},{8,24},{16,0},{24,8},{1,17},{9,25},{17,1},{25,9},{2,18},{10... | collective-permute-start | bytes 786440 | tf_op jit(solution)/shard_map/ppermute | solution.py:35
  309.8 13.3 %collective-permute-start.25 = (bf16[64,2048]{1,0:T(8,128)(2,1)S(1)}, bf16[64,2048]{1,0:T(8,128)(2,1)S(1)}, u32[]{:S(2)}, u32[]{:S(2)}) collective-permute-start(bf16[64,2048]{1,0:T(8,128)(2,1)S(1)} %collective-permute-done.24), channel_id=1, source_target_pairs={{0,16},{8,24},{16,0},{24,8},{1,17},{9,25},{17,1},{25,9},{2,18},{10... | collective-permute-start | bytes 786440 | tf_op jit(solution)/shard_map/ppermute | solution.py:35
  313.0 76.1 %collective-permute-start.50 = (bf16[64,2048]{1,0:T(8,128)(2,1)S(1)}, bf16[64,2048]{1,0:T(8,128)(2,1)S(1)}, u32[]{:S(2)}, u32[]{:S(2)}) collective-permute-start(bf16[64,2048]{1,0:T(8,128)(2,1)S(1)} %get-tuple-element.38), channel_id=1, source_target_pairs={{0,4},{1,5},{2,6},{3,7},{4,0},{5,1},{6,2},{7,3},{8,12},{9,13},{10,... | collective-permute-start | bytes 786440 | tf_op jit(solution)/shard_map/ppermute | solution.py:35
  321.6 57.6 %collective-permute-start.66 = (bf16[64,2048]{1,0:T(8,128)(2,1)S(1)}, bf16[64,2048]{1,0:T(8,128)(2,1)S(1)}, u32[]{:S(2)}, u32[]{:S(2)}) collective-permute-start(bf16[64,2048]{1,0:T(8,128)(2,1)S(1)} %collective-permute-done.64), channel_id=1, source_target_pairs={{0,1},{1,0},{2,3},{3,2},{4,5},{5,4},{6,7},{7,6},{8,9},{9,8},{10,11... | collective-permute-start | bytes 786440 | tf_op jit(solution)/shard_map/ppermute | solution.py:35
  389.1 14.5 %collective-permute-start.36 = (bf16[64,2048]{1,0:T(8,128)(2,1)S(1)}, bf16[64,2048]{1,0:T(8,128)(2,1)S(1)}, u32[]{:S(2)}, u32[]{:S(2)}) collective-permute-start(bf16[64,2048]{1,0:T(8,128)(2,1)S(1)} %get-tuple-element.38), channel_id=1, source_target_pairs={{0,2},{1,3},{2,0},{3,1},{4,6},{5,7},{6,4},{7,5},{8,10},{9,11},{10,... | collective-permute-start | bytes 786440 | tf_op jit(solution)/shard_map/ppermute | solution.py:35
  389.2 14.7 %collective-permute-start.52 = (bf16[64,2048]{1,0:T(8,128)(2,1)S(1)}, bf16[64,2048]{1,0:T(8,128)(2,1)S(1)}, u32[]{:S(2)}, u32[]{:S(2)}) collective-permute-start(bf16[64,2048]{1,0:T(8,128)(2,1)S(1)} %collective-permute-done.50), channel_id=1, source_target_pairs={{0,1},{1,0},{2,3},{3,2},{4,5},{5,4},{6,7},{7,6},{8,9},{9,8},{10,11... | collective-permute-start | bytes 786440 | tf_op jit(solution)/shard_map/ppermute | solution.py:35
  415.9 14.5 %collective-permute-start.37 = (bf16[64,2048]{1,0:T(8,128)(2,1)S(1)}, bf16[64,2048]{1,0:T(8,128)(2,1)S(1)}, u32[]{:S(2)}, u32[]{:S(2)}) collective-permute-start(bf16[64,2048]{1,0:T(8,128)(2,1)S(1)} %collective-permute-done.36), channel_id=1, source_target_pairs={{0,16},{8,24},{16,0},{24,8},{1,17},{9,25},{17,1},{25,9},{2,18},{10... | collective-permute-start | bytes 786440 | tf_op jit(solution)/shard_map/ppermute | solution.py:35
  482.8 17.5 %collective-permute-start.68 = (bf16[128,2048]{1,0:T(8,128)(2,1)S(1)}, bf16[128,2048]{1,0:T(8,128)(2,1)S(1)}, u32[]{:S(2)}, u32[]{:S(2)}) collective-permute-start(bf16[128,2048]{1,0:T(8,128)(2,1)S(1)} %slice.598), channel_id=1, source_target_pairs={{0,1},{1,0},{2,3},{3,2},{4,5},{5,4},{6,7},{7,6},{8,9},{9,8},{10,11... | collective-permute-start | bytes 1572872 | tf_op jit(solution)/shard_map/ppermute | solution.py:35
  482.9 20.6 %collective-permute-start.54 = (bf16[128,2048]{1,0:T(8,128)(2,1)S(1)}, bf16[128,2048]{1,0:T(8,128)(2,1)S(1)}, u32[]{:S(2)}, u32[]{:S(2)}) collective-permute-start(bf16[128,2048]{1,0:T(8,128)(2,1)S(1)} %slice.582), channel_id=1, source_target_pairs={{0,1},{1,0},{2,3},{3,2},{4,5},{5,4},{6,7},{7,6},{8,9},{9,8},{10,11... | collective-permute-start | bytes 1572872 | tf_op jit(solution)/shard_map/ppermute | solution.py:35
  484.9 30.3 %collective-permute-start.57 = (bf16[128,2048]{1,0:T(8,128)(2,1)S(1)}, bf16[128,2048]{1,0:T(8,128)(2,1)S(1)}, u32[]{:S(2)}, u32[]{:S(2)}) collective-permute-start(bf16[128,2048]{1,0:T(8,128)(2,1)S(1)} %pad_maximum_fusion.5), channel_id=1, source_target_pairs={{0,16},{8,24},{16,0},{24,8},{1,17},{9,25},{17,1},{25,9},{2,18},{10... | collective-permute-start | bytes 1572872 | tf_op jit(solution)/shard_map/ppermute | solution.py:35
  486.2 23.7 %collective-permute-start.40 = (bf16[128,2048]{1,0:T(8,128)(2,1)S(1)}, bf16[128,2048]{1,0:T(8,128)(2,1)S(1)}, u32[]{:S(2)}, u32[]{:S(2)}) collective-permute-start(bf16[128,2048]{1,0:T(8,128)(2,1)S(1)} %slice.566), channel_id=1, source_target_pairs={{0,1},{1,0},{2,3},{3,2},{4,5},{5,4},{6,7},{7,6},{8,9},{9,8},{10,11... | collective-permute-start | bytes 1572872 | tf_op jit(solution)/shard_map/ppermute | solution.py:35
  500.0 14.9 %collective-permute-start.71 = (bf16[128,2048]{1,0:T(8,128)(2,1)S(1)}, bf16[128,2048]{1,0:T(8,128)(2,1)S(1)}, u32[]{:S(2)}, u32[]{:S(2)}) collective-permute-start(bf16[128,2048]{1,0:T(8,128)(2,1)S(1)} %pad_maximum_fusion.6), channel_id=1, source_target_pairs={{0,16},{8,24},{16,0},{24,8},{1,17},{9,25},{17,1},{25,9},{2,18},{10... | collective-permute-start | bytes 1572872 | tf_op jit(solution)/shard_map/ppermute | solution.py:35
  500.3 24.0 %collective-permute-start.43 = (bf16[128,2048]{1,0:T(8,128)(2,1)S(1)}, bf16[128,2048]{1,0:T(8,128)(2,1)S(1)}, u32[]{:S(2)}, u32[]{:S(2)}) collective-permute-start(bf16[128,2048]{1,0:T(8,128)(2,1)S(1)} %pad_maximum_fusion.4), channel_id=1, source_target_pairs={{0,16},{8,24},{16,0},{24,8},{1,17},{9,25},{17,1},{25,9},{2,18},{10... | collective-permute-start | bytes 1572872 | tf_op jit(solution)/shard_map/ppermute | solution.py:35
  503.5 22.1 %collective-permute-start.28 = (bf16[128,2048]{1,0:T(8,128)(2,1)S(1)}, bf16[128,2048]{1,0:T(8,128)(2,1)S(1)}, u32[]{:S(2)}, u32[]{:S(2)}) collective-permute-start(bf16[128,2048]{1,0:T(8,128)(2,1)S(1)} %slice.550), channel_id=1, source_target_pairs={{0,1},{1,0},{2,3},{3,2},{4,5},{5,4},{6,7},{7,6},{8,9},{9,8},{10,11... | collective-permute-start | bytes 1572872 | tf_op jit(solution)/shard_map/ppermute | solution.py:35
  509.9 20.1 %collective-permute-start.30 = (bf16[128,2048]{1,0:T(8,128)(2,1)S(1)}, bf16[128,2048]{1,0:T(8,128)(2,1)S(1)}, u32[]{:S(2)}, u32[]{:S(2)}) collective-permute-start(bf16[128,2048]{1,0:T(8,128)(2,1)S(1)} %pad_maximum_fusion.3), channel_id=1, source_target_pairs={{0,16},{8,24},{16,0},{24,8},{1,17},{9,25},{17,1},{25,9},{2,18},{10... | collective-permute-start | bytes 1572872 | tf_op jit(solution)/shard_map/ppermute | solution.py:35
  514.8 17.9 %collective-permute-start.69 = (bf16[64,2048]{1,0:T(8,128)(2,1)S(1)}, bf16[64,2048]{1,0:T(8,128)(2,1)S(1)}, u32[]{:S(2)}, u32[]{:S(2)}) collective-permute-start(bf16[64,2048]{1,0:T(8,128)(2,1)S(1)} %slice.600), channel_id=1, source_target_pairs={{0,16},{8,24},{16,0},{24,8},{1,17},{9,25},{17,1},{25,9},{2,18},{10... | collective-permute-start | bytes 786440 | tf_op jit(solution)/shard_map/ppermute | solution.py:35
  515.3 18.9 %collective-permute-start.72 = (bf16[64,2048]{1,0:T(8,128)(2,1)S(1)}, bf16[64,2048]{1,0:T(8,128)(2,1)S(1)}, u32[]{:S(2)}, u32[]{:S(2)}) collective-permute-start(bf16[64,2048]{1,0:T(8,128)(2,1)S(1)} %slice.606), channel_id=1, source_target_pairs={{0,1},{1,0},{2,3},{3,2},{4,5},{5,4},{6,7},{7,6},{8,9},{9,8},{10,11... | collective-permute-start | bytes 786440 | tf_op jit(solution)/shard_map/ppermute | solution.py:35
  538.3 16.8 %collective-permute-start.73 = (bf16[64,2048]{1,0:T(8,128)(2,1)S(1)}, bf16[64,2048]{1,0:T(8,128)(2,1)S(1)}, u32[]{:S(2)}, u32[]{:S(2)}) collective-permute-start(bf16[64,2048]{1,0:T(8,128)(2,1)S(1)} %add_convert_fusion.11), channel_id=1, source_target_pairs={{0,6},{1,7},{2,4},{3,5},{4,2},{5,3},{6,0},{7,1},{8,14},{9,15},{10,... | collective-permute-start | bytes 786440 | tf_op jit(solution)/shard_map/ppermute | solution.py:35
  541.1 19.1 %collective-permute-start.56 = (bf16[64,2048]{1,0:T(8,128)(2,1)S(1)}, bf16[64,2048]{1,0:T(8,128)(2,1)S(1)}, u32[]{:S(2)}, u32[]{:S(2)}) collective-permute-start(bf16[64,2048]{1,0:T(8,128)(2,1)S(1)} %add_convert_fusion.14), channel_id=1, source_target_pairs={{0,4},{1,5},{2,6},{3,7},{4,0},{5,1},{6,2},{7,3},{8,12},{9,13},{10,... | collective-permute-start | bytes 786440 | tf_op jit(solution)/shard_map/ppermute | solution.py:35
  542.1 21.0 %collective-permute-start.59 = (bf16[64,2048]{1,0:T(8,128)(2,1)S(1)}, bf16[64,2048]{1,0:T(8,128)(2,1)S(1)}, u32[]{:S(2)}, u32[]{:S(2)}) collective-permute-start(bf16[64,2048]{1,0:T(8,128)(2,1)S(1)} %add_convert_fusion.13), channel_id=1, source_target_pairs={{0,4},{1,5},{2,6},{3,7},{4,0},{5,1},{6,2},{7,3},{8,12},{9,13},{10,... | collective-permute-start | bytes 786440 | tf_op jit(solution)/shard_map/ppermute | solution.py:35
  544.3 18.7 %collective-permute-start.42 = (bf16[64,2048]{1,0:T(8,128)(2,1)S(1)}, bf16[64,2048]{1,0:T(8,128)(2,1)S(1)}, u32[]{:S(2)}, u32[]{:S(2)}) collective-permute-start(bf16[64,2048]{1,0:T(8,128)(2,1)S(1)} %add_convert_fusion.16), channel_id=1, source_target_pairs={{0,2},{1,3},{2,0},{3,1},{4,6},{5,7},{6,4},{7,5},{8,10},{9,11},{10,... | collective-permute-start | bytes 786440 | tf_op jit(solution)/shard_map/ppermute | solution.py:35
  545.3 19.7 %collective-permute-start.45 = (bf16[64,2048]{1,0:T(8,128)(2,1)S(1)}, bf16[64,2048]{1,0:T(8,128)(2,1)S(1)}, u32[]{:S(2)}, u32[]{:S(2)}) collective-permute-start(bf16[64,2048]{1,0:T(8,128)(2,1)S(1)} %add_convert_fusion.15), channel_id=1, source_target_pairs={{0,2},{1,3},{2,0},{3,1},{4,6},{5,7},{6,4},{7,5},{8,10},{9,11},{10,... | collective-permute-start | bytes 786440 | tf_op jit(solution)/shard_map/ppermute | solution.py:35
  (84 other events, 1163.5 us)
